TPU v7x, 32 devices: a whole 2x2x4 slice. The times are simulated.
32 devices in a mesh: groups: 2 (over x), dp: 16 (over z, y, core).
Axes of the slice: x: 2, y: 2, z: 4, core: 2. Of those that a mesh axis runs over, the one named last changes fastest.
Arguments:
- inputs: bfloat16 [8192, 4096], P(('groups', 'dp')), parts along dimension 0, may hold values from -6 to 6
- gate_values: bfloat16 [8192, 4096], P(('groups', 'dp')), parts along dimension 0, may hold values from -6 to 6
- write_proj: bfloat16 [8192, 128], P(('groups', 'dp')), parts along dimension 0, may hold values from -6 to 6
- read_proj: bfloat16 [8192, 128], P(('groups', 'dp')), parts along dimension 0, may hold values from -0.59765625 to 0.59765625
- step_raw: bfloat16 [8192, 64], P(('groups', 'dp')), parts along dimension 0, may hold values from -3 to 10
- cotangent: bfloat16 [8192, 4096], P(('groups', 'dp')), parts along dimension 0, may hold values from -6 to 6
- step_bias: float32 [64], replicated, may hold values from -5.5 to -3.5
- rate_log: float32 [64], replicated
- skip_gain: float32 [64], replicated, may hold values from 0.5 to 1.5
- norm_gain: float32 [4096], replicated, may hold values from 0.5 to 1.5
- state_bank: bfloat16 [128, 64, 64, 128], P('groups', 'dp'), parts along dimension 0, may hold values from -1.796875 to 1.796875
- turn_index: int32 [8192], P(('groups', 'dp')), parts along dimension 0, may hold values from 0 to 3, as said below
- turn_slot: int32 [128], P('groups'), parts along dimension 0, may hold values from 0 to 63, each once
Outputs:
- grad_inputs: bfloat16 [8192, 4096], P(('groups', 'dp')), parts along dimension 0
- state_grad: bfloat16 [128, 64, 64, 128], P('groups', 'dp'), parts along dimension 0
- gain_grad: float32 [8192], P(('groups', 'dp')), parts along dimension 0
- head_grads: float32 [6, 64], P('groups'), parts along dimension 0
There are 2 independent parts, one for each index of `groups`. A program takes and returns all parts, laid end to end along the dimension named above; an argument that names none is the same for every part. Nothing has to cross between parts.
Inputs may be any that keep to these rules, and one draw needn't show every extreme that they name: `turn_index`: within each device's 256 tokens turn numbers start at 0, never fall and rise by one at each new turn; some device has 4 turns. `turn_slot`: each slot number appears once.
All inputs are finite; a program needn't handle non-finite values.
Results may differ from a plain program's by a relative error of at most 0.0051.
Values may be sent and summed in bfloat16 or wider, within the bound.
No kernel may reach another device: no remote copies, remote signals or barrier semaphores. Data moves between devices by JAX's collectives and lax.ppermute only.
A program may use at most 128 MiB of HBM per device.

v0:
```python
import jax
import jax.numpy as jnp
from jax import lax
from jax.sharding import PartitionSpec as P

HDIM = 64
DSTATE = 128
BLOCK_LEN = 256
TMAX = 4


def project_turns(states, read_proj, turn_index):
    turn_cap = states.shape[0]
    onehot = turn_index[:, None] == jnp.arange(turn_cap, dtype=jnp.int32)[None, :]
    masked = jnp.where(onehot[:, :, None], read_proj[:, None, :], jnp.zeros((), read_proj.dtype))
    return jnp.einsum("tgn,ghpn->thp", masked, states, preferred_element_type=jnp.float32).astype(
        jnp.bfloat16
    )


def turn_grads(read_grad, read_proj, turn_index, turn_cap):
    onehot = turn_index[:, None] == jnp.arange(turn_cap, dtype=jnp.int32)[None, :]
    masked = jnp.where(onehot[:, :, None], read_proj[:, None, :], jnp.zeros((), read_proj.dtype))
    return jnp.einsum("tgn,thp->ghpn", masked, read_grad, preferred_element_type=jnp.float32)


def mixer(
    input_value,
    start_read,
    bias_value,
    rate_value,
    skip_value,
    gain_value,
    gate_values,
    write_proj,
    read_proj,
    step_raw,
    turn_index,
):
    row_count = input_value.shape[0]
    head_count = step_raw.shape[1]
    head_dim = input_value.shape[1] // head_count
    state_dim = write_proj.shape[1]
    block_count = row_count // BLOCK_LEN
    highest = lax.Precision.HIGHEST
    step_size = jax.nn.softplus(step_raw.astype(jnp.float32) + bias_value[None, :])
    log_decay = -jnp.exp(rate_value)[None, :] * step_size
    starts = jnp.concatenate([jnp.ones((1,), jnp.bool_), turn_index[1:] != turn_index[:-1]])
    blocked = (
        input_value.reshape(block_count, BLOCK_LEN, head_count, head_dim),
        write_proj.reshape(block_count, BLOCK_LEN, state_dim),
        read_proj.reshape(block_count, BLOCK_LEN, state_dim),
        step_size.reshape(block_count, BLOCK_LEN, head_count),
        log_decay.reshape(block_count, BLOCK_LEN, head_count),
        turn_index.reshape(block_count, BLOCK_LEN),
        starts.reshape(block_count, BLOCK_LEN),
        start_read.reshape(block_count, BLOCK_LEN, head_count, head_dim),
    )
    token_positions = jnp.arange(BLOCK_LEN, dtype=jnp.int32)
    causal_mask = token_positions[:, None] >= token_positions[None, :]

    def advance(carried, pieces):
        state_now, since_now = carried
        (
            block_x,
            block_write,
            block_read,
            block_step,
            block_decay,
            block_turn,
            block_start,
            block_begin,
        ) = pieces
        running = jnp.cumsum(block_decay, axis=0)
        before = running - block_decay
        same_mask = (causal_mask & (block_turn[:, None] == block_turn[None, :]))[:, :, None]
        decay_mat = jnp.exp(jnp.where(same_mask, running[:, None, :] - running[None, :, :], -1e30))
        offset = jnp.max(jnp.where(same_mask, before[None, :, :], -1e30), axis=1)
        scores = jnp.dot(block_read, block_write.T, preferred_element_type=jnp.float32)
        weights = decay_mat * scores[:, :, None] * block_step[None, :, :]
        local_part = jnp.einsum("tsh,shp->thp", weights, block_x, precision=highest)
        kept = ((block_turn == block_turn[0]) & jnp.logical_not(block_start[0])).astype(jnp.float32)
        inner = running - offset
        read_f = block_read.astype(jnp.float32)
        projected = jnp.einsum("hpn,tn->thp", state_now, read_f, precision=highest)
        since = inner + kept[:, None] * since_now[None, :]
        carry_factor = jnp.exp(inner) * kept[:, None]
        output = (
            local_part
            + carry_factor[:, :, None] * projected
            + jnp.exp(since)[:, :, None] * block_begin
            + skip_value[None, :, None] * block_x
        )
        last_weights = decay_mat[-1] * block_step
        new_state = carry_factor[-1][:, None, None] * state_now + jnp.einsum(
            "sh,shp,sn->hpn",
            last_weights,
            block_x,
            block_write.astype(jnp.float32),
            precision=highest,
        )
        return ((new_state, since[-1]), output)

    start_state = (
        jnp.zeros((head_count, head_dim, state_dim), jnp.float32),
        jnp.zeros((head_count,), jnp.float32),
    )
    final_state, outputs = lax.scan(advance, start_state, blocked)
    mixed = outputs.reshape(row_count, head_count, head_dim)
    gate_f = gate_values.astype(jnp.float32).reshape(row_count, head_count, head_dim)
    gated_out = mixed * jax.nn.silu(gate_f)
    mean_square = jnp.mean(gated_out * gated_out, axis=-1, keepdims=True)
    normed = (
        gated_out * lax.rsqrt(mean_square + 1e-05) * gain_value.reshape(head_count, head_dim)[None]
    )
    return normed.reshape(row_count, head_count * head_dim)


def learner(
    inputs,
    start_read,
    step_bias,
    rate_log,
    skip_gain,
    norm_gain,
    gate_values,
    write_proj,
    read_proj,
    step_raw,
    turn_index,
    cotangent,
):

    def forward(input_value, read_value, bias_value, rate_value, skip_value, gain_value):
        return mixer(
            input_value,
            read_value,
            bias_value,
            rate_value,
            skip_value,
            gain_value,
            gate_values,
            write_proj,
            read_proj,
            step_raw,
            turn_index,
        )

    primal, pullback = jax.vjp(
        forward,
        inputs.astype(jnp.float32),
        start_read.astype(jnp.float32),
        step_bias,
        rate_log,
        skip_gain,
        norm_gain,
    )
    return pullback(cotangent.astype(jnp.float32))


def local(
    inputs,
    gate_values,
    write_proj,
    read_proj,
    step_raw,
    cotangent,
    step_bias,
    rate_log,
    skip_gain,
    norm_gain,
    state_bank,
    turn_index,
    turn_slot,
):
    devices = lax.axis_size("dp")
    inverse = jnp.argsort(turn_slot)
    head_part = state_bank.shape[1]
    row_count = inputs.shape[0]
    position = lax.axis_index("dp")
    moved_inputs, moved_gates, moved_cot, moved_steps = (
        lax.all_to_all(inputs, "dp", split_axis=1, concat_axis=0, tiled=True),
        lax.all_to_all(gate_values, "dp", split_axis=1, concat_axis=0, tiled=True),
        lax.all_to_all(cotangent, "dp", split_axis=1, concat_axis=0, tiled=True),
        lax.all_to_all(step_raw, "dp", split_axis=1, concat_axis=0, tiled=True),
    )
    write_all, read_all = (
        lax.all_gather(write_proj, "dp", axis=0, tiled=True),
        lax.all_gather(read_proj, "dp", axis=0, tiled=True),
    )
    turns_all = lax.all_gather(turn_index, "dp", axis=0, tiled=True)
    start_head = position * head_part
    own_bias = lax.dynamic_slice_in_dim(step_bias, start_head, head_part)
    own_rate = lax.dynamic_slice_in_dim(rate_log, start_head, head_part)
    own_skip = lax.dynamic_slice_in_dim(skip_gain, start_head, head_part)
    own_gain = lax.dynamic_slice_in_dim(norm_gain, start_head * HDIM, head_part * HDIM)
    initial = state_bank[turn_slot].reshape(devices, TMAX, head_part, HDIM, DSTATE)

    def split_rows(value):
        return value.reshape((devices, row_count) + value.shape[1:])

    read_split = split_rows(read_all)
    turns_split = split_rows(turns_all)
    start_read = jax.vmap(project_turns)(initial, read_split, turns_split)
    batched = jax.vmap(learner, in_axes=(0, 0, None, None, None, None, 0, 0, 0, 0, 0, 0))
    gradients = batched(
        split_rows(moved_inputs),
        start_read,
        own_bias,
        own_rate,
        own_skip,
        own_gain,
        split_rows(moved_gates),
        split_rows(write_all),
        read_split,
        split_rows(moved_steps),
        turns_split,
        split_rows(moved_cot),
    )
    grad_local = gradients[0].reshape(devices * row_count, head_part * HDIM).astype(jnp.bfloat16)
    grad_inputs = lax.all_to_all(grad_local, "dp", split_axis=0, concat_axis=1, tiled=True)
    read_grad = gradients[1].astype(jnp.bfloat16)
    holder_turns = jax.vmap(turn_grads, in_axes=(0, 0, 0, None))(
        read_grad, read_split, turns_split, TMAX
    )
    state_grad = holder_turns.reshape(devices * TMAX, head_part, HDIM, DSTATE).astype(jnp.bfloat16)[
        inverse
    ]
    own_heads = jnp.stack(
        [
            jnp.sum(gradients[2], axis=0),
            jnp.sum(gradients[3], axis=0),
            jnp.sum(gradients[4], axis=0),
        ]
    )
    head_grads = lax.all_gather(own_heads, "dp", axis=1, tiled=True)
    gain_grad = jnp.sum(gradients[5], axis=0)
    return (grad_inputs, state_grad, gain_grad, head_grads)


def solution(mesh):
    in_specs = (
        P(("groups", "dp"), None),
        P(("groups", "dp"), None),
        P(("groups", "dp"), None),
        P(("groups", "dp"), None),
        P(("groups", "dp"), None),
        P(("groups", "dp"), None),
        P(),
        P(),
        P(),
        P(),
        P("groups", "dp", None, None),
        P(("groups", "dp")),
        P("groups"),
    )
    out_specs = (
        P(("groups", "dp"), None),
        P("groups", "dp", None, None),
        P(("groups", "dp")),
        P("groups", None),
    )
    return jax.shard_map(local, mesh=mesh, in_specs=in_specs, out_specs=out_specs, check_vma=False)
```

profile of v0, /device:TPU:9, one launch (start us, length us, event | category | flops | bytes accessed | tf_op | source)
XLA Modules:
  0.0 391.7 jit_solution(12096214340189381911)
XLA Ops:
  8.6 6.6 %all-to-all-start = ((bf16[256,16,4]{0,2,1:T(4,128)(2,1)}), bf16[256,16,4]{0,2,1:T(4,128)(2,1)S(1)}, u32[]{:S(2)}, u32[]{:S(2)}) async-start(bf16[256,16,4]{0,2,1:T(4,128)(2,1)} %all_to_all.54), calls=%async_computation | async-start | bytes 65536 | tf_op jit(solution)/shard_map/all_to_all | solution.py:185
  15.1 4.1 %copy.107 = bf16[256,4096]{0,1:T(8,128)(2,1)} copy(bf16[256,4096]{1,0:T(8,128)(2,1)} %param.14) | data formatting | bytes 4194304 | tf_op jit(solution)/shard_map/all_to_all | solution.py:183
  20.2 5.2 %all-to-all-start.3 = ((bf16[256,16,256]{0,2,1:T(8,128)(2,1)}), bf16[256,16,256]{0,2,1:T(8,128)(2,1)S(1)}, u32[]{:S(2)}, u32[]{:S(2)}) async-start(bf16[256,16,256]{0,2,1:T(8,128)(2,1)} %bitcast.249), calls=%async_computation.3 | async-start | bytes 4194304 | tf_op jit(solution)/shard_map/all_to_all | solution.py:183
  26.2 4.1 %copy.106 = bf16[256,4096]{0,1:T(8,128)(2,1)} copy(bf16[256,4096]{1,0:T(8,128)(2,1)} %param.13) | data formatting | bytes 4194304 | tf_op jit(solution)/shard_map/all_to_all | solution.py:182
  30.3 46.6 %all-to-all-done.3 = bf16[256,16,256]{0,2,1:T(8,128)(2,1)S(1)} async-done(((bf16[256,16,256]{0,2,1:T(8,128)(2,1)}), bf16[256,16,256]{0,2,1:T(8,128)(2,1)S(1)}, u32[]{:S(2)}, u32[]{:S(2)}) %all-to-all-start.3) | async-done | bytes 2097184 | tf_op jit(solution)/shard_map/all_to_all | solution.py:183
  76.9 6.9 %all-to-all-start.2 = ((bf16[256,16,256]{0,2,1:T(8,128)(2,1)}), bf16[256,16,256]{0,2,1:T(8,128)(2,1)}, u32[]{:S(2)}, u32[]{:S(2)}) async-start(bf16[256,16,256]{0,2,1:T(8,128)(2,1)} %bitcast.247), calls=%async_computation.2 | async-start | bytes 4194304 | tf_op jit(solution)/shard_map/all_to_all | solution.py:182
  84.6 63.3 %all-gather = s32[16,1,256]{2,1,0:T(1,128)S(1)} all-gather(s32[1,1,256]{2,1,0:T(1,128)S(1)} %bitcast.271), channel_id=1, replica_groups=mesh['groups'=2,'dp'=16] {'dp'}, dimensions={0}, use_global_device_ids=true | all-gather | bytes 17408 | tf_op jit(solution)/shard_map/all_gather | solution.py:191
  149.4 4.1 %copy.105 = bf16[256,4096]{0,1:T(8,128)(2,1)} copy(bf16[256,4096]{1,0:T(8,128)(2,1)} %param.18) | data formatting | bytes 4194304 | tf_op jit(solution)/shard_map/all_to_all | solution.py:184
  153.4 5.3 %gather_fusion = bf16[64,4,64,128]{3,2,1,0:T(8,128)(2,1)} fusion(bf16[64,4,64,128]{3,2,1,0:T(8,128)(2,1)} %param.23, s32[1024]{0:T(1024)S(1)} %pad_clamp_fusion.1), kind=kCustom, calls=%fused_computation | custom fusion | bytes 8388864 | tf_op jit(solution)/shard_map/gather | solution.py:197
  160.5 2.3 reduce-window.26
  163.3 4.9 %fusion.64 = f32[16,4,64,256]{3,2,1,0:T(8,128)} fusion(bf16[16,256,128,1]{2,1,3,0:T(8,128)(2,1)} %bitcast.253), kind=kOutput, calls=%fused_computation.90 | convolution fusion | flops 1610612736 | bytes 5242880 | tf_op jit(solution)/shard_map/vmap(jvp())/while/body/eval_jaxpr/hpn,tn->thp/dot_general | solution.py:85
  168.2 4.3 %fusion.99 = f32[16,256,256]{2,1,0:T(8,128)} fusion(bf16[16,256,128]{2,1,0:T(8,128)(2,1)} %bitcast.254, bf16[16,256,128]{2,1,0:T(8,128)(2,1)} %bitcast.257), kind=kOutput, calls=%fused_computation.162 | convolution fusion | flops 268435456 | bytes 6291456 | tf_op jit(solution)/shard_map/vmap(jvp())/while/body/eval_jaxpr/dot_general | solution.py:79
  172.6 5.7 %bitcast_convert_fusion = bf16[16,256,4,64]{1,3,2,0:T(8,128)(2,1)} fusion(bf16[16,4,4,64,128]{4,3,2,1,0:T(8,128)(2,1)S(1)} %bitcast.252, pred[16,256,4]{1,2,0:T(4,128)(4,1)S(1)} %iota_compare_fusion.1, bf16[16,256,128]{2,1,0:T(8,128)(2,1)S(1)} %bitcast.255), kind=kOutput, calls=%fused_computation.52 | convolution fusion | flops 1076887552 | bytes 7356416 | tf_op jit(solution)/shard_map/vmap(tgn,ghpn->thp)/dot_general | solution.py:16
  178.3 2.4 convert_element_type.148
  180.7 4.0 %all-to-all-start.1 = ((bf16[256,16,256]{0,2,1:T(8,128)(2,1)}), bf16[256,16,256]{0,2,1:T(8,128)(2,1)S(1)}, u32[]{:S(2)}, u32[]{:S(2)}) async-start(bf16[256,16,256]{0,2,1:T(8,128)(2,1)} %bitcast.248), calls=%async_computation.1 | async-start | bytes 4194304 | tf_op jit(solution)/shard_map/all_to_all | solution.py:184
  184.7 6.2 %fusion.48 = (f32[16,256,4]{1,2,0:T(4,128)S(1)}, f32[16,4,64,256]{3,2,1,0:T(8,128)}) fusion(bf16[256,16,256]{0,2,1:T(8,128)(2,1)} %all-to-all-done.2, bf16[16,256,128,1]{2,1,3,0:T(8,128)(2,1)} %bitcast.258), kind=kOutput, calls=%fused_computation.73 | convolution fusion | flops 1613742080 | bytes 7405568 | tf_op jit(solution)/shard_map/vmap(transpose(jvp()))/while/body/eval_jaxpr/sh,shp,sn->hpn/dot_general | solution.py:95
  191.8 2.4 select_reduce_fusion
  196.3 16.8 %multiply_reduce_fusion.2 = (f32[16,256,4]{1,2,0:T(4,128)S(1)}, f32[16,256,4,64]{1,3,2,0:T(8,128)}, f32[16,256,4,64]{1,3,2,0:T(8,128)}) fusion(f32[16,256,4,64]{1,3,2,0:T(8,128)S(1)} %bitcast.250, f32[16,256,4,64]{1,3,2,0:T(8,128)S(1)} %bitcast.251, f32[4]{0:T(128)S(1)} %copy-done.36, bf16[16,256,4,64]{1,3,2,0:T(8,128)(2,1)S(1)} %copy-done.12, ...), kind=kOutput, calls=%fused_computation.78 | convolution fusion | flops 3252666368 | bytes 30736400 | tf_op jit(solution)/shard_map/vmap(jvp())/while/body/eval_jaxpr/tsh,shp->thp/dot_general | solution.py:81
  213.2 5.9 %fusion.2 = f32[16,256,4]{1,2,0:T(4,128)} fusion(f32[16,256,4]{1,2,0:T(4,128)S(1)} %select_reduce_fusion, f32[16,256,4]{1,2,0:T(4,128)S(1)} %get-tuple-element.439, pred[16,256,256]{2,1,0:T(8,128)(4,1)S(1)} %compare_and_fusion), kind=kLoop, calls=%fused_computation.6 | loop fusion | flops 16760832 | bytes 1245184 | tf_op jit(solution)/shard_map/vmap(jvp())/while/body/eval_jaxpr/reduce_sum | solution.py:78
  219.1 11.7 %all-to-all-done.1 = bf16[256,16,256]{0,2,1:T(8,128)(2,1)S(1)} async-done(((bf16[256,16,256]{0,2,1:T(8,128)(2,1)}), bf16[256,16,256]{0,2,1:T(8,128)(2,1)S(1)}, u32[]{:S(2)}, u32[]{:S(2)}) %all-to-all-start.1) | async-done | bytes 2097184 | tf_op jit(solution)/shard_map/all_to_all | solution.py:184
  233.0 2.4 multiply_reduce_fusion
  236.5 3.8 fusion.46
  240.4 28.3 %fusion.28 = (f32[16,256,4]{1,2,0:T(4,128)S(1)}, f32[16,256,4]{1,2,0:T(4,128)S(1)}, f32[16,256,4]{1,2,0:T(4,128)}, f32[16,256,4]{1,2,0:T(4,128)S(1)}, f32[16,256,256,4]{2,1,3,0:T(8,128)}) fusion(f32[16,256,4]{1,2,0:T(4,128)S(1)} %bitcast.261, f32[16,256,256]{2,1,0:T(8,128)S(1)} %copy-done.7, f32[16,256,4]{1,2,0:T(4,128)S(1)} %copy-done.23, ...), kind=kOutput, calls=%fused_computation.42 | convolution fusion | flops 3292463104 | bytes 28966912 | tf_op jit(solution)/shard_map/vmap(transpose(jvp()))/while/body/eval_jaxpr/tsh,shp->thp/dot_general | solution.py:81
  269.5 9.9 %reduce-window.28 = f32[16,4,2,128]{3,0,1,2:T(8,128)S(1)} reduce-window(f32[16,4,2,128]{3,0,1,2:T(8,128)S(1)} %copy.91, f32[]{:T(128)} %constant.180.clone.1), window={size=1x1x1x128 pad=0_0x0_0x0_0x0_127}, to_apply=%region_14.15 | reduce-window | flops 2080768 | bytes 131076 | tf_op jit(solution)/shard_map/reduce-window
  282.8 19.1 %fusion.38 = bf16[16,256,4,64]{1,3,2,0:T(8,128)(2,1)} fusion(f32[16,4,64,256]{3,2,1,0:T(8,128)} %get-tuple-element.442, f32[16,256,4,64]{1,3,2,0:T(8,128)} %copy-done.5, f32[4]{0:T(128)} %dynamic_slice.104, f32[16,256,4]{1,2,0:T(4,128)S(1)} %get-tuple-element.437, f32[16,256,4]{1,2,0:T(4,128)} %copy-done.22, f32[16,256,256]{2,1,0:T(8,128)} %fusion.99, ...), kind=kOutput, calls=%fused_computation.57 | convolution fusion | flops 3243245568 | bytes 15925264 | tf_op jit(solution)/shard_map/vmap(transpose(jvp()))/while/body/eval_jaxpr/tsh,shp->thp/dot_general | solution.py:81
  301.9 6.3 %all-to-all-start.4 = ((bf16[16,256,256]{1,2,0:T(8,128)(2,1)}), bf16[16,256,256]{1,2,0:T(8,128)(2,1)}, u32[]{:S(2)}, u32[]{:S(2)}) async-start(bf16[16,256,256]{1,2,0:T(8,128)(2,1)} %bitcast.259), calls=%async_computation.4 | async-start | bytes 4194304 | tf_op jit(solution)/shard_map/all_to_all | solution.py:221
  310.3 5.0 %fusion.37 = f32[256]{0:T(256)S(1)} fusion(f32[16,256,4,64]{1,3,2,0:T(8,128)} %get-tuple-element.443, f32[256]{0:T(256)S(1)} %dynamic_slice.105, f32[16,256,4]{1,2,0:T(4,128)S(1)} %multiply_multiply_fusion, f32[16,256,4]{1,2,0:T(4,128)S(1)} %fusion.87, bf16[256,16,256]{0,2,1:T(8,128)(2,1)} %all-to-all-done.2, bf16[256,16,256]{0,2,1:T(8,128)(2,1)} %copy-done, ...), kind=kLoop, calls=%fused_computation.51 | loop fusion | flops 16776960 | bytes 10618880 | tf_op jit(solution)/shard_map/reduce_sum | solution.py:233
  315.8 50.2 %all-gather.1 = f32[16,4,3]{2,1,0:T(4,128)S(1)} all-gather(f32[1,4,3]{2,1,0:T(4,128)S(1)} %bitcast.266), channel_id=1, replica_groups=mesh['groups'=2,'dp'=16] {'dp'}, dimensions={0}, use_global_device_ids=true | all-gather | bytes 816 | tf_op jit(solution)/shard_map/all_gather | solution.py:236
  366.7 5.3 %convert_bitcast_fusion = bf16[16,4,4,64,128]{4,3,1,2,0:T(8,128)(2,1)S(1)} fusion(pred[16,256,4]{1,2,0:T(4,128)(4,1)S(1)} %copy-done.25, f32[16,256,4,64]{1,3,2,0:T(8,128)} %copy-done.5, bf16[16,256,128]{2,1,0:T(8,128)(2,1)S(1)} %bitcast.256, f32[16,256,4]{1,2,0:T(4,128)S(1)} %copy-done.19), kind=kOutput, calls=%fused_computation.75 | convolution fusion | flops 1080033280 | bytes 9519104 | tf_op jit(solution)/shard_map/vmap(tgn,thp->ghpn)/dot_general | solution.py:24
  371.9 2.9 copy.89
  375.5 5.3 %gather_fusion.1 = bf16[64,4,64,128]{3,2,1,0:T(8,128)(2,1)} fusion(bf16[64,4,64,128]{3,2,1,0:T(8,128)(2,1)} %bitcast.246, s32[1024]{0:T(1024)S(1)} %pad_clamp_fusion), kind=kCustom, calls=%fused_computation.1 | custom fusion | bytes 8388864 | tf_op jit(solution)/shard_map/gather | solution.py:226
  380.8 4.1 %copy.108 = bf16[256,4096]{1,0:T(8,128)(2,1)} copy(bf16[256,4096]{0,1:T(8,128)(2,1)} %bitcast.33) | data formatting | bytes 4194304 | tf_op jit(solution)/shard_map/all_to_all | solution.py:221
  (135 shorter events, 21.8 us)
Async XLA Ops:
  8.6 11.6 %all-to-all-start = ((bf16[256,16,4]{0,2,1:T(4,128)(2,1)}), bf16[256,16,4]{0,2,1:T(4,128)(2,1)S(1)}, u32[]{:S(2)}, u32[]{:S(2)}) async-start(bf16[256,16,4]{0,2,1:T(4,128)(2,1)} %all_to_all.54), calls=%async_computation | async-start | bytes 65536 | tf_op jit(solution)/shard_map/all_to_all | solution.py:185
  20.2 170.8 %copy-start.14 = (bf16[256,16,4]{0,2,1:T(4,128)(2,1)}, bf16[256,16,4]{0,2,1:T(4,128)(2,1)S(1)}, u32[]{:S(2)}) copy-start(bf16[256,16,4]{0,2,1:T(4,128)(2,1)S(1)} %all-to-all-done) | copy-start | bytes 98308
  20.2 56.7 %all-to-all-start.3 = ((bf16[256,16,256]{0,2,1:T(8,128)(2,1)}), bf16[256,16,256]{0,2,1:T(8,128)(2,1)S(1)}, u32[]{:S(2)}, u32[]{:S(2)}) async-start(bf16[256,16,256]{0,2,1:T(8,128)(2,1)} %bitcast.249), calls=%async_computation.3 | async-start | bytes 4194304 | tf_op jit(solution)/shard_map/all_to_all | solution.py:183
  25.4 137.9 %all-gather.7.cloned.1.call-start = ((), (), s32[]{:S(2)}) async-start(), calls=%async_computation.6 | async-start | bytes 1114112 | tf_op jit(solution)/shard_map/all_gather | solution.py:189
  26.1 58.4 %copy-start.34 = (s32[64]{0:T(128)S(1)}, s32[64]{0:T(128)}, u32[]{:S(2)}) copy-start(s32[64]{0:T(128)} %param.25) | copy-start | bytes 772
  26.1 58.4 %copy-start.30 = (s32[256]{0:T(256)S(1)}, s32[256]{0:T(256)}, u32[]{:S(2)}) copy-start(s32[256]{0:T(256)} %param.24) | copy-start | bytes 3076
  26.2 121.7 %copy-start.32 = (f32[64]{0:T(128)S(1)}, f32[64]{0:T(128)}, u32[]{:S(2)}) copy-start(f32[64]{0:T(128)} %param.19) | copy-start | bytes 772
  26.2 121.8 %copy-start.33 = (f32[64]{0:T(128)S(1)}, f32[64]{0:T(128)}, u32[]{:S(2)}) copy-start(f32[64]{0:T(128)} %param.21) | copy-start | bytes 772
  76.9 101.4 %copy-start = (bf16[256,16,256]{0,2,1:T(8,128)(2,1)}, bf16[256,16,256]{0,2,1:T(8,128)(2,1)S(1)}, u32[]{:S(2)}) copy-start(bf16[256,16,256]{0,2,1:T(8,128)(2,1)S(1)} %all-to-all-done.3) | copy-start | bytes 6291460
  76.9 103.8 %all-to-all-start.2 = ((bf16[256,16,256]{0,2,1:T(8,128)(2,1)}), bf16[256,16,256]{0,2,1:T(8,128)(2,1)}, u32[]{:S(2)}, u32[]{:S(2)}) async-start(bf16[256,16,256]{0,2,1:T(8,128)(2,1)} %bitcast.247), calls=%async_computation.2 | async-start | bytes 4194304 | tf_op jit(solution)/shard_map/all_to_all | solution.py:182
  83.8 84.4 %all-gather.5.cloned.1.call-start = ((), (), s32[]{:S(2)}) async-start(), calls=%async_computation.5 | async-start | bytes 1114112 | tf_op jit(solution)/shard_map/all_gather | solution.py:188
  147.9 43.0 %copy-start.27 = (f32[4]{0:T(128)}, f32[4]{0:T(128)S(1)}, u32[]{:S(2)}) copy-start(f32[4]{0:T(128)S(1)} %dynamic_slice.103) | copy-start | bytes 52
  153.4 5.3 %copy-start.31 = (f32[64]{0:T(128)S(1)}, f32[64]{0:T(128)}, u32[]{:S(2)}) copy-start(f32[64]{0:T(128)} %param.20) | copy-start | bytes 772
  159.4 13.2 %copy-start.24 = (pred[16,256,4]{1,2,0:T(4,128)(4,1)}, pred[16,256,4]{1,2,0:T(4,128)(4,1)S(1)}, u32[]{:S(2)}) copy-start(pred[16,256,4]{1,2,0:T(4,128)(4,1)S(1)} %iota_compare_fusion.1) | copy-start | bytes 49156
  168.2 4.3 %copy-start.10 = (bf16[4096,128]{1,0:T(8,128)(2,1)S(1)}, bf16[4096,128]{1,0:T(8,128)(2,1)}, u32[]{:S(2)}) copy-start(bf16[4096,128]{1,0:T(8,128)(2,1)} %all-gather.7.cloned.1.call-done) | copy-start | bytes 3145732
  180.7 50.1 %all-to-all-start.1 = ((bf16[256,16,256]{0,2,1:T(8,128)(2,1)}), bf16[256,16,256]{0,2,1:T(8,128)(2,1)S(1)}, u32[]{:S(2)}, u32[]{:S(2)}) async-start(bf16[256,16,256]{0,2,1:T(8,128)(2,1)} %bitcast.248), calls=%async_computation.1 | async-start | bytes 4194304 | tf_op jit(solution)/shard_map/all_to_all | solution.py:184
  184.7 11.6 %copy-start.6 = (f32[16,256,256]{2,1,0:T(8,128)S(1)}, f32[16,256,256]{2,1,0:T(8,128)}, u32[]{:S(2)}) copy-start(f32[16,256,256]{2,1,0:T(8,128)} %fusion.99) | copy-start | bytes 12582916
  184.7 11.6 %copy-start.8 = (f32[256,16,256]{0,2,1:T(8,128)S(1)}, f32[256,16,256]{0,2,1:T(8,128)}, u32[]{:S(2)}) copy-start(f32[256,16,256]{0,2,1:T(8,128)} %convert_element_type.148) | copy-start | bytes 12582916
  190.9 5.4 %copy-start.3 = (f32[16,4,64,256]{3,2,1,0:T(8,128)S(1)}, f32[16,4,64,256]{3,2,1,0:T(8,128)}, u32[]{:S(2)}) copy-start(f32[16,4,64,256]{3,2,1,0:T(8,128)} %fusion.64) | copy-start | bytes 12582916
  190.9 5.4 %copy-start.12 = (bf16[16,256,4,64]{1,3,2,0:T(8,128)(2,1)S(1)}, bf16[16,256,4,64]{1,3,2,0:T(8,128)(2,1)}, u32[]{:S(2)}) copy-start(bf16[16,256,4,64]{1,3,2,0:T(8,128)(2,1)} %bitcast_convert_fusion) | copy-start | bytes 6291460
  190.9 5.4 %copy-start.36 = (f32[4]{0:T(128)S(1)}, f32[4]{0:T(128)}, u32[]{:S(2)}) copy-start(f32[4]{0:T(128)} %dynamic_slice.104) | copy-start | bytes 52
  191.8 21.4 %copy-start.22 = (f32[16,256,4]{1,2,0:T(4,128)}, f32[16,256,4]{1,2,0:T(4,128)S(1)}, u32[]{:S(2)}) copy-start(f32[16,256,4]{1,2,0:T(4,128)S(1)} %get-tuple-element.440) | copy-start | bytes 196612
  194.2 19.0 %copy-start.17 = (f32[16,256,4]{1,2,0:T(4,128)}, f32[16,256,4]{1,2,0:T(4,128)S(1)}, u32[]{:S(2)}) copy-start(f32[16,256,4]{1,2,0:T(4,128)S(1)} %get-tuple-element.433) | copy-start | bytes 196612
  213.2 22.2 %copy-start.16 = (f32[16,256,4]{1,2,0:T(4,128)}, f32[16,256,4]{1,2,0:T(4,128)S(1)}, u32[]{:S(2)}) copy-start(f32[16,256,4]{1,2,0:T(4,128)S(1)} %get-tuple-element.430) | copy-start | bytes 196612
  240.3 28.4 %copy-start.5 = (f32[16,256,4,64]{1,3,2,0:T(8,128)}, f32[16,256,4,64]{1,3,2,0:T(8,128)S(1)}, u32[]{:S(2)}) copy-start(f32[16,256,4,64]{1,3,2,0:T(8,128)S(1)} %get-tuple-element.429) | copy-start | bytes 12582916
  301.9 6.3 %copy-start.35 = (s32[64]{0:T(128)S(1)}, s32[64]{0:T(128)}, u32[]{:S(2)}) copy-start(s32[64]{0:T(128)} %param.25) | copy-start | bytes 772
  301.9 78.8 %all-to-all-start.4 = ((bf16[16,256,256]{1,2,0:T(8,128)(2,1)}), bf16[16,256,256]{1,2,0:T(8,128)(2,1)}, u32[]{:S(2)}, u32[]{:S(2)}) async-start(bf16[16,256,256]{1,2,0:T(8,128)(2,1)} %bitcast.259), calls=%async_computation.4 | async-start | bytes 4194304 | tf_op jit(solution)/shard_map/all_to_all | solution.py:221
  310.2 5.3 %copy-start.29 = (f32[4]{0:T(128)S(1)}, f32[4]{0:T(128)}, u32[]{:S(2)}) copy-start(f32[4]{0:T(128)} %get-tuple-element.435) | copy-start | bytes 52
  310.2 5.5 %copy-start.28 = (f32[4]{0:T(128)S(1)}, f32[4]{0:T(128)}, u32[]{:S(2)}) copy-start(f32[4]{0:T(128)} %get-tuple-element.427) | copy-start | bytes 52
  310.3 56.4 %copy-start.11 = (bf16[4096,128]{1,0:T(8,128)(2,1)S(1)}, bf16[4096,128]{1,0:T(8,128)(2,1)}, u32[]{:S(2)}) copy-start(bf16[4096,128]{1,0:T(8,128)(2,1)} %all-gather.7.cloned.1.call-done) | copy-start | bytes 3145732
  310.3 56.4 %copy-start.19 = (f32[16,256,4]{1,2,0:T(4,128)S(1)}, f32[16,256,4]{1,2,0:T(4,128)}, u32[]{:S(2)}) copy-start(f32[16,256,4]{1,2,0:T(4,128)} %copy-done.17) | copy-start | bytes 196612
  310.3 56.4 %copy-start.25 = (pred[16,256,4]{1,2,0:T(4,128)(4,1)S(1)}, pred[16,256,4]{1,2,0:T(4,128)(4,1)}, u32[]{:S(2)}) copy-start(pred[16,256,4]{1,2,0:T(4,128)(4,1)} %copy-done.24) | copy-start | bytes 49156
  (12 other events, 39.5 us)
Sparse Core Ops, SparseCore 0:
  28.4 51.8 all-gather.6
  86.8 51.8 all-gather.4
where the time goes:
time: 393 us; the launch traced here: 392 us
  blocking collectives  113 us (29%)
  matrix products  90.7 us (23%)
  waiting for transfers between devices  60.7 us (15%)
  other arithmetic  44.7 us (11%)
  local copies, waits for them, and re-layouts  38.5 us (10%)
  starting transfers between devices  29 us (7%)
  between operations  14.7 us (4%)
    dot_general x3, matrix products, advance(): local_part = jnp.einsum('tsh,shp->thp', weights, block_x, precision=highest)  64.2 us
    all_gather x1, blocking collectives, local(): turns_all = lax.all_gather(turn_index, 'dp', axis=0, tiled=True)  63.3 us
    all_gather x1, blocking collectives, local(): head_grads = lax.all_gather(own_heads, 'dp', axis=1, tiled=True)  50.2 us
    all_to_all x1, waiting for transfers between devices, local(): lax.all_to_all(gate_values, 'dp', split_axis=1, concat_axis=0, tiled=True)  46.6 us
    another operation x5, other arithmetic  12.3 us
    all_to_all x1, waiting for transfers between devices, local(): lax.all_to_all(cotangent, 'dp', split_axis=1, concat_axis=0, tiled=True)  11.7 us
  transfers between devices with their start and end apart: 7, of which 3 were waited for; matrix products, arithmetic and copies ran while one was open for 25% of the time, Pallas kernels for 0%

commit v1 on v0

--- a/solution.py
+++ b/solution.py
@@ -7,6 +7,22 @@
 DSTATE = 128
 BLOCK_LEN = 256
 TMAX = 4
+
+
+def gather_around(x, axis, dim):
+    ways, here, turn = (lax.axis_size(axis), lax.axis_index(axis), x.shape[dim])
+    shape = [n * ways if d == dim else n for d, n in enumerate(x.shape)]
+    full = lax.dynamic_update_slice_in_dim(jnp.zeros(shape, x.dtype), x, here * turn, axis=dim)
+    going_up = going_down = x
+    for far in range(1, ways // 2 + 1):
+        going_up = lax.ppermute(going_up, axis, [(d, (d + 1) % ways) for d in range(ways)])
+        full = lax.dynamic_update_slice_in_dim(full, going_up, (here - far) % ways * turn, axis=dim)
+        if 2 * far < ways:
+            going_down = lax.ppermute(going_down, axis, [(d, (d - 1) % ways) for d in range(ways)])
+            full = lax.dynamic_update_slice_in_dim(
+                full, going_down, (here + far) % ways * turn, axis=dim
+            )
+    return full
 
 
 def project_turns(states, read_proj, turn_index):
@@ -188,7 +204,7 @@
         lax.all_gather(write_proj, "dp", axis=0, tiled=True),
         lax.all_gather(read_proj, "dp", axis=0, tiled=True),
     )
-    turns_all = lax.all_gather(turn_index, "dp", axis=0, tiled=True)
+    turns_all = gather_around(turn_index, "dp", 0)
     start_head = position * head_part
     own_bias = lax.dynamic_slice_in_dim(step_bias, start_head, head_part)
     own_rate = lax.dynamic_slice_in_dim(rate_log, start_head, head_part)

time: 393 us -> 413 us (1.051)
  starting transfers between devices: 29 us -> 95.9 us
  blocking collectives: 113 us -> 50.2 us
  waiting for transfers between devices: 60.7 us -> 69.2 us
    all_gather x1 -> x0, blocking collectives: 63.3 us -> none  [local(): turns_all = lax.all_gather(turn_index, 'dp', axis=0, tiled=True)]
    ppermute x0 -> x15, starting transfers between devices: none -> 62.2 us  [the longest x8 34.8 us: gather_around(): lax.ppermute(going_up, axis, [(d, (d + 1) % ways) for d in range(ways)])]
    ppermute x0 -> x15, waiting for transfers between devices: none -> 9.36 us  [the longest x8 7.93 us: gather_around(): lax.ppermute(going_up, axis, [(d, (d + 1) % ways) for d in range(ways)])]
    all_to_all x1, starting transfers between devices: 3.99 us -> 8.7 us  [local(): lax.all_to_all(cotangent, 'dp', split_axis=1, concat_axis=0, tiled=True)]
  transfers between devices with their start and end apart: 7 -> 22, of which waited for: 3 -> 13; matrix products, arithmetic and copies ran while one was open for 25% -> 25% of each run, Pallas kernels for 0% -> 0%
where the time goes in v1:
time: 413 us; the launch traced here: 408 us
  starting transfers between devices  95.9 us (23%)
  matrix products  90.8 us (22%)
  waiting for transfers between devices  69.2 us (17%)
  blocking collectives  50.2 us (12%)
  other arithmetic  44.6 us (11%)
  local copies, waits for them, and re-layouts  42.3 us (10%)
  between operations  15 us (4%)
    dot_general x3, matrix products, advance(): local_part = jnp.einsum('tsh,shp->thp', weights, block_x, precision=highest)  64.3 us
    all_gather x1, blocking collectives, local(): head_grads = lax.all_gather(own_heads, 'dp', axis=1, tiled=True)  50.2 us
    all_to_all x1, waiting for transfers between devices, local(): lax.all_to_all(gate_values, 'dp', split_axis=1, concat_axis=0, tiled=True)  46.6 us
    ppermute x8, starting transfers between devices, gather_around(): lax.ppermute(going_up, axis, [(d, (d + 1) % ways) for d in range(ways)])  34.8 us
    ppermute x7, starting transfers between devices, gather_around(): lax.ppermute(going_down, axis, [(d, (d - 1) % ways) for d in range(ways)])  27.4 us
    another operation x5, other arithmetic  12.3 us
    all_to_all x1, waiting for transfers between devices, local(): lax.all_to_all(cotangent, 'dp', split_axis=1, concat_axis=0, tiled=True)  11.6 us
    all_to_all x1, starting transfers between devices, local(): lax.all_to_all(cotangent, 'dp', split_axis=1, concat_axis=0, tiled=True)  8.7 us
  transfers between devices with their start and end apart: 22, of which 13 were waited for; matrix products, arithmetic and copies ran while one was open for 25% of the time, Pallas kernels for 0%

profile of v1, /device:TPU:9, one launch (start us, length us, event | category | flops | bytes accessed | tf_op | source)
XLA Modules:
  0.0 407.9 jit_solution(7416059005860521515)
XLA Ops:
  8.6 6.6 %all-to-all-start = ((bf16[256,16,4]{0,2,1:T(4,128)(2,1)}), bf16[256,16,4]{0,2,1:T(4,128)(2,1)S(1)}, u32[]{:S(2)}, u32[]{:S(2)}) async-start(bf16[256,16,4]{0,2,1:T(4,128)(2,1)} %all_to_all.54), calls=%async_computation | async-start | bytes 65536 | tf_op jit(solution)/shard_map/all_to_all | solution.py:201
  15.1 4.1 copy.107
  20.2 5.2 %all-to-all-start.3 = ((bf16[256,16,256]{0,2,1:T(8,128)(2,1)}), bf16[256,16,256]{0,2,1:T(8,128)(2,1)S(1)}, u32[]{:S(2)}, u32[]{:S(2)}) async-start(bf16[256,16,256]{0,2,1:T(8,128)(2,1)} %bitcast.245), calls=%async_computation.3 | async-start | bytes 4194304 | tf_op jit(solution)/shard_map/all_to_all | solution.py:199
  26.2 4.1 %copy.106 = bf16[256,4096]{0,1:T(8,128)(2,1)} copy(bf16[256,4096]{1,0:T(8,128)(2,1)} %param.13) | data formatting | bytes 4194304 | tf_op jit(solution)/shard_map/all_to_all | solution.py:198
  30.3 46.6 %all-to-all-done.3 = bf16[256,16,256]{0,2,1:T(8,128)(2,1)S(1)} async-done(((bf16[256,16,256]{0,2,1:T(8,128)(2,1)}), bf16[256,16,256]{0,2,1:T(8,128)(2,1)S(1)}, u32[]{:S(2)}, u32[]{:S(2)}) %all-to-all-start.3) | async-done | bytes 2097184 | tf_op jit(solution)/shard_map/all_to_all | solution.py:199
  76.9 6.9 %all-to-all-start.2 = ((bf16[256,16,256]{0,2,1:T(8,128)(2,1)}), bf16[256,16,256]{0,2,1:T(8,128)(2,1)}, u32[]{:S(2)}, u32[]{:S(2)}) async-start(bf16[256,16,256]{0,2,1:T(8,128)(2,1)} %bitcast.243), calls=%async_computation.2 | async-start | bytes 4194304 | tf_op jit(solution)/shard_map/all_to_all | solution.py:198
  86.1 6.4 %collective-permute-done = s32[256]{0:T(256)S(1)} collective-permute-done((s32[256]{0:T(256)S(1)}, s32[256]{0:T(256)S(1)}, u32[]{:S(2)}, u32[]{:S(2)}) %collective-permute-start) | collective-permute-done | bytes 1056 | tf_op jit(solution)/shard_map/ppermute | solution.py:18
  95.0 27.4 %collective-permute-start.3 = (s32[256]{0:T(256)S(1)}, s32[256]{0:T(256)S(1)}, u32[]{:S(2)}, u32[]{:S(2)}) collective-permute-start(s32[256]{0:T(256)S(1)} %collective-permute-done.1), channel_id=1, source_target_pairs={{0,15},{1,0},{2,1},{3,2},{4,3},{5,4},{6,5},{7,6},{8,7},{9,8},{10,9... | collective-permute-start | bytes 3080 | tf_op jit(solution)/shard_map/ppermute | solution.py:21
  123.0 14.4 %collective-permute-start.4 = (s32[256]{0:T(256)S(1)}, s32[256]{0:T(256)S(1)}, u32[]{:S(2)}, u32[]{:S(2)}) collective-permute-start(s32[256]{0:T(256)S(1)} %collective-permute-done.2), channel_id=1, source_target_pairs={{0,1},{1,2},{2,3},{3,4},{4,5},{5,6},{6,7},{7,8},{8,9},{9,10},{10,1... | collective-permute-start | bytes 3080 | tf_op jit(solution)/shard_map/ppermute | solution.py:18
  138.1 3.5 collective-permute-start.6
  142.4 3.2 collective-permute-start.8
  154.4 4.1 %copy.105 = bf16[256,4096]{0,1:T(8,128)(2,1)} copy(bf16[256,4096]{1,0:T(8,128)(2,1)} %param.18) | data formatting | bytes 4194304 | tf_op jit(solution)/shard_map/all_to_all | solution.py:200
  158.5 3.4 collective-permute-start.14
  161.9 5.3 %gather_fusion = bf16[64,4,64,128]{3,2,1,0:T(8,128)(2,1)} fusion(bf16[64,4,64,128]{3,2,1,0:T(8,128)(2,1)} %param.23, s32[1024]{0:T(1024)S(1)} %pad_clamp_fusion.1), kind=kCustom, calls=%fused_computation | custom fusion | bytes 8388864 | tf_op jit(solution)/shard_map/gather | solution.py:213
  174.7 5.0 %fusion.64 = f32[16,4,64,256]{3,2,1,0:T(8,128)} fusion(bf16[16,256,128,1]{2,1,3,0:T(8,128)(2,1)} %bitcast.249), kind=kOutput, calls=%fused_computation.90 | convolution fusion | flops 1610612736 | bytes 5242880 | tf_op jit(solution)/shard_map/vmap(jvp())/while/body/eval_jaxpr/hpn,tn->thp/dot_general | solution.py:101
  179.7 4.3 %fusion.99 = f32[16,256,256]{2,1,0:T(8,128)} fusion(bf16[16,256,128]{2,1,0:T(8,128)(2,1)} %bitcast.250, bf16[16,256,128]{2,1,0:T(8,128)(2,1)} %bitcast.253), kind=kOutput, calls=%fused_computation.161 | convolution fusion | flops 268435456 | bytes 6291456 | tf_op jit(solution)/shard_map/vmap(jvp())/while/body/eval_jaxpr/dot_general | solution.py:95
  184.0 5.7 %bitcast_convert_fusion = bf16[16,256,4,64]{1,3,2,0:T(8,128)(2,1)} fusion(bf16[16,4,4,64,128]{4,3,2,1,0:T(8,128)(2,1)S(1)} %bitcast.248, pred[16,256,4]{1,2,0:T(4,128)(4,1)S(1)} %iota_compare_fusion.1, bf16[16,256,128]{2,1,0:T(8,128)(2,1)S(1)} %bitcast.251), kind=kOutput, calls=%fused_computation.52 | convolution fusion | flops 1076887552 | bytes 7356416 | tf_op jit(solution)/shard_map/vmap(tgn,ghpn->thp)/dot_general | solution.py:32
  192.2 8.7 %all-to-all-start.1 = ((bf16[256,16,256]{0,2,1:T(8,128)(2,1)}), bf16[256,16,256]{0,2,1:T(8,128)(2,1)S(1)}, u32[]{:S(2)}, u32[]{:S(2)}) async-start(bf16[256,16,256]{0,2,1:T(8,128)(2,1)} %bitcast.244), calls=%async_computation.1 | async-start | bytes 4194304 | tf_op jit(solution)/shard_map/all_to_all | solution.py:200
  200.9 6.2 %fusion.48 = (f32[16,256,4]{1,2,0:T(4,128)S(1)}, f32[16,4,64,256]{3,2,1,0:T(8,128)}) fusion(bf16[256,16,256]{0,2,1:T(8,128)(2,1)} %all-to-all-done.2, bf16[16,256,128,1]{2,1,3,0:T(8,128)(2,1)} %bitcast.254), kind=kOutput, calls=%fused_computation.73 | convolution fusion | flops 1613742080 | bytes 7405568 | tf_op jit(solution)/shard_map/vmap(transpose(jvp()))/while/body/eval_jaxpr/sh,shp,sn->hpn/dot_general | solution.py:111
  212.5 16.9 %multiply_reduce_fusion.2 = (f32[16,256,4]{1,2,0:T(4,128)S(1)}, f32[16,256,4,64]{1,3,2,0:T(8,128)}, f32[16,256,4,64]{1,3,2,0:T(8,128)}) fusion(f32[16,256,4,64]{1,3,2,0:T(8,128)S(1)} %bitcast.246, f32[16,256,4,64]{1,3,2,0:T(8,128)S(1)} %bitcast.247, f32[4]{0:T(128)S(1)} %copy-done.36, bf16[16,256,4,64]{1,3,2,0:T(8,128)(2,1)S(1)} %copy-done.12, ...), kind=kOutput, calls=%fused_computation.78 | convolution fusion | flops 3252666368 | bytes 30736400 | tf_op jit(solution)/shard_map/vmap(jvp())/while/body/eval_jaxpr/tsh,shp->thp/dot_general | solution.py:97
  229.4 5.8 %fusion.2 = f32[16,256,4]{1,2,0:T(4,128)} fusion(f32[16,256,4]{1,2,0:T(4,128)S(1)} %select_reduce_fusion, f32[16,256,4]{1,2,0:T(4,128)S(1)} %get-tuple-element.439, pred[16,256,256]{2,1,0:T(8,128)(4,1)S(1)} %compare_and_fusion), kind=kLoop, calls=%fused_computation.6 | loop fusion | flops 16760832 | bytes 1245184 | tf_op jit(solution)/shard_map/vmap(jvp())/while/body/eval_jaxpr/reduce_sum | solution.py:94
  235.3 11.6 %all-to-all-done.1 = bf16[256,16,256]{0,2,1:T(8,128)(2,1)S(1)} async-done(((bf16[256,16,256]{0,2,1:T(8,128)(2,1)}), bf16[256,16,256]{0,2,1:T(8,128)(2,1)S(1)}, u32[]{:S(2)}, u32[]{:S(2)}) %all-to-all-start.1) | async-done | bytes 2097184 | tf_op jit(solution)/shard_map/all_to_all | solution.py:200
  252.6 3.8 fusion.46
  256.5 28.3 %fusion.28 = (f32[16,256,4]{1,2,0:T(4,128)S(1)}, f32[16,256,4]{1,2,0:T(4,128)S(1)}, f32[16,256,4]{1,2,0:T(4,128)}, f32[16,256,4]{1,2,0:T(4,128)S(1)}, f32[16,256,256,4]{2,1,3,0:T(8,128)}) fusion(f32[16,256,4]{1,2,0:T(4,128)S(1)} %bitcast.257, f32[16,256,256]{2,1,0:T(8,128)S(1)} %copy-done.7, f32[16,256,4]{1,2,0:T(4,128)S(1)} %copy-done.23, ...), kind=kOutput, calls=%fused_computation.42 | convolution fusion | flops 3292463104 | bytes 28966912 | tf_op jit(solution)/shard_map/vmap(transpose(jvp()))/while/body/eval_jaxpr/tsh,shp->thp/dot_general | solution.py:97
  285.6 9.9 %reduce-window.28 = f32[16,4,2,128]{3,0,1,2:T(8,128)S(1)} reduce-window(f32[16,4,2,128]{3,0,1,2:T(8,128)S(1)} %copy.91, f32[]{:T(128)} %constant.263.clone.1), window={size=1x1x1x128 pad=0_0x0_0x0_0x0_127}, to_apply=%region_14.15 | reduce-window | flops 2080768 | bytes 131076 | tf_op jit(solution)/shard_map/reduce-window
  298.8 19.1 %fusion.38 = bf16[16,256,4,64]{1,3,2,0:T(8,128)(2,1)} fusion(f32[16,4,64,256]{3,2,1,0:T(8,128)} %get-tuple-element.442, f32[16,256,4,64]{1,3,2,0:T(8,128)} %copy-done.5, f32[4]{0:T(128)} %dynamic_slice.104, f32[16,256,4]{1,2,0:T(4,128)S(1)} %get-tuple-element.437, f32[16,256,4]{1,2,0:T(4,128)} %copy-done.22, f32[16,256,256]{2,1,0:T(8,128)} %fusion.99, ...), kind=kOutput, calls=%fused_computation.57 | convolution fusion | flops 3243245568 | bytes 15925264 | tf_op jit(solution)/shard_map/vmap(transpose(jvp()))/while/body/eval_jaxpr/tsh,shp->thp/dot_general | solution.py:97
  318.0 6.2 %all-to-all-start.4 = ((bf16[16,256,256]{1,2,0:T(8,128)(2,1)}), bf16[16,256,256]{1,2,0:T(8,128)(2,1)}, u32[]{:S(2)}, u32[]{:S(2)}) async-start(bf16[16,256,256]{1,2,0:T(8,128)(2,1)} %bitcast.255), calls=%async_computation.4 | async-start | bytes 4194304 | tf_op jit(solution)/shard_map/all_to_all | solution.py:237
  326.3 5.0 %fusion.37 = f32[256]{0:T(256)S(1)} fusion(f32[16,256,4,64]{1,3,2,0:T(8,128)} %get-tuple-element.443, f32[256]{0:T(256)S(1)} %dynamic_slice.105, f32[16,256,4]{1,2,0:T(4,128)S(1)} %multiply_multiply_fusion, f32[16,256,4]{1,2,0:T(4,128)S(1)} %fusion.87, bf16[256,16,256]{0,2,1:T(8,128)(2,1)} %all-to-all-done.2, bf16[256,16,256]{0,2,1:T(8,128)(2,1)} %copy-done, ...), kind=kLoop, calls=%fused_computation.51 | loop fusion | flops 16776960 | bytes 10618880 | tf_op jit(solution)/shard_map/reduce_sum | solution.py:249
  331.9 50.2 %all-gather = f32[16,4,3]{2,1,0:T(4,128)S(1)} all-gather(f32[1,4,3]{2,1,0:T(4,128)S(1)} %bitcast.260), channel_id=1, replica_groups=mesh['groups'=2,'dp'=16] {'dp'}, dimensions={0}, use_global_device_ids=true | all-gather | bytes 816 | tf_op jit(solution)/shard_map/all_gather | solution.py:252
  382.7 5.3 %convert_bitcast_fusion = bf16[16,4,4,64,128]{4,3,1,2,0:T(8,128)(2,1)S(1)} fusion(pred[16,256,4]{1,2,0:T(4,128)(4,1)S(1)} %copy-done.25, f32[16,256,4,64]{1,3,2,0:T(8,128)} %copy-done.5, bf16[16,256,128]{2,1,0:T(8,128)(2,1)S(1)} %bitcast.252, f32[16,256,4]{1,2,0:T(4,128)S(1)} %copy-done.19), kind=kOutput, calls=%fused_computation.75 | convolution fusion | flops 1080033280 | bytes 9519104 | tf_op jit(solution)/shard_map/vmap(tgn,thp->ghpn)/dot_general | solution.py:40
  391.5 5.3 %gather_fusion.1 = bf16[64,4,64,128]{3,2,1,0:T(8,128)(2,1)} fusion(bf16[64,4,64,128]{3,2,1,0:T(8,128)(2,1)} %bitcast.242, s32[1024]{0:T(1024)S(1)} %pad_clamp_fusion), kind=kCustom, calls=%fused_computation.1 | custom fusion | bytes 8388864 | tf_op jit(solution)/shard_map/gather | solution.py:242
  396.8 4.1 copy.108
  (181 shorter events, 50.4 us)
Async XLA Ops:
  8.6 11.6 %all-to-all-start = ((bf16[256,16,4]{0,2,1:T(4,128)(2,1)}), bf16[256,16,4]{0,2,1:T(4,128)(2,1)S(1)}, u32[]{:S(2)}, u32[]{:S(2)}) async-start(bf16[256,16,4]{0,2,1:T(4,128)(2,1)} %all_to_all.54), calls=%async_computation | async-start | bytes 65536 | tf_op jit(solution)/shard_map/all_to_all | solution.py:201
  20.2 187.0 %copy-start.14 = (bf16[256,16,4]{0,2,1:T(4,128)(2,1)}, bf16[256,16,4]{0,2,1:T(4,128)(2,1)S(1)}, u32[]{:S(2)}) copy-start(bf16[256,16,4]{0,2,1:T(4,128)(2,1)S(1)} %all-to-all-done) | copy-start | bytes 98308
  20.2 56.7 %all-to-all-start.3 = ((bf16[256,16,256]{0,2,1:T(8,128)(2,1)}), bf16[256,16,256]{0,2,1:T(8,128)(2,1)S(1)}, u32[]{:S(2)}, u32[]{:S(2)}) async-start(bf16[256,16,256]{0,2,1:T(8,128)(2,1)} %bitcast.245), calls=%async_computation.3 | async-start | bytes 4194304 | tf_op jit(solution)/shard_map/all_to_all | solution.py:199
  25.4 149.3 %all-gather.6.cloned.1.call-start = ((), (), s32[]{:S(2)}) async-start(), calls=%async_computation.6 | async-start | bytes 1114112 | tf_op jit(solution)/shard_map/all_gather | solution.py:205
  26.1 57.7 %copy-start.30 = (s32[256]{0:T(256)S(1)}, s32[256]{0:T(256)}, u32[]{:S(2)}) copy-start(s32[256]{0:T(256)} %param.24) | copy-start | bytes 3076
  26.1 59.3 %copy-start.34 = (s32[64]{0:T(128)S(1)}, s32[64]{0:T(128)}, u32[]{:S(2)}) copy-start(s32[64]{0:T(128)} %param.25) | copy-start | bytes 772
  26.2 59.3 %copy-start.31 = (f32[64]{0:T(128)S(1)}, f32[64]{0:T(128)}, u32[]{:S(2)}) copy-start(f32[64]{0:T(128)} %param.20) | copy-start | bytes 772
  26.2 123.3 %copy-start.32 = (f32[64]{0:T(128)S(1)}, f32[64]{0:T(128)}, u32[]{:S(2)}) copy-start(f32[64]{0:T(128)} %param.19) | copy-start | bytes 772
  26.2 123.4 %copy-start.33 = (f32[64]{0:T(128)S(1)}, f32[64]{0:T(128)}, u32[]{:S(2)}) copy-start(f32[64]{0:T(128)} %param.21) | copy-start | bytes 772
  76.9 112.9 %copy-start = (bf16[256,16,256]{0,2,1:T(8,128)(2,1)}, bf16[256,16,256]{0,2,1:T(8,128)(2,1)S(1)}, u32[]{:S(2)}) copy-start(bf16[256,16,256]{0,2,1:T(8,128)(2,1)S(1)} %all-to-all-done.3) | copy-start | bytes 6291460
  76.9 115.3 %all-to-all-start.2 = ((bf16[256,16,256]{0,2,1:T(8,128)(2,1)}), bf16[256,16,256]{0,2,1:T(8,128)(2,1)}, u32[]{:S(2)}, u32[]{:S(2)}) async-start(bf16[256,16,256]{0,2,1:T(8,128)(2,1)} %bitcast.243), calls=%async_computation.2 | async-start | bytes 4194304 | tf_op jit(solution)/shard_map/all_to_all | solution.py:198
  83.8 95.9 %all-gather.4.cloned.1.call-start = ((), (), s32[]{:S(2)}) async-start(), calls=%async_computation.5 | async-start | bytes 1114112 | tf_op jit(solution)/shard_map/all_gather | solution.py:204
  83.8 8.6 %collective-permute-start = (s32[256]{0:T(256)S(1)}, s32[256]{0:T(256)S(1)}, u32[]{:S(2)}, u32[]{:S(2)}) collective-permute-start(s32[256]{0:T(256)S(1)} %copy-done.30), channel_id=1, source_target_pairs={{0,1},{1,2},{2,3},{3,4},{4,5},{5,6},{6,7},{7,8},{8,9},{9,10},{10,1... | collective-permute-start | bytes 3080 | tf_op jit(solution)/shard_map/ppermute | solution.py:18
  85.4 9.6 %collective-permute-start.1 = (s32[256]{0:T(256)S(1)}, s32[256]{0:T(256)S(1)}, u32[]{:S(2)}, u32[]{:S(2)}) collective-permute-start(s32[256]{0:T(256)S(1)} %copy-done.30), channel_id=1, source_target_pairs={{0,15},{1,0},{2,1},{3,2},{4,3},{5,4},{6,5},{7,6},{8,7},{9,8},{10,9... | collective-permute-start | bytes 3080 | tf_op jit(solution)/shard_map/ppermute | solution.py:21
  92.5 30.6 %collective-permute-start.2 = (s32[256]{0:T(256)S(1)}, s32[256]{0:T(256)S(1)}, u32[]{:S(2)}, u32[]{:S(2)}) collective-permute-start(s32[256]{0:T(256)S(1)} %collective-permute-done), channel_id=1, source_target_pairs={{0,1},{1,2},{2,3},{3,4},{4,5},{5,6},{6,7},{7,8},{8,9},{9,10},{10,1... | collective-permute-start | bytes 3080 | tf_op jit(solution)/shard_map/ppermute | solution.py:18
  95.0 42.9 %collective-permute-start.3 = (s32[256]{0:T(256)S(1)}, s32[256]{0:T(256)S(1)}, u32[]{:S(2)}, u32[]{:S(2)}) collective-permute-start(s32[256]{0:T(256)S(1)} %collective-permute-done.1), channel_id=1, source_target_pairs={{0,15},{1,0},{2,1},{3,2},{4,3},{5,4},{6,5},{7,6},{8,7},{9,8},{10,9... | collective-permute-start | bytes 3080 | tf_op jit(solution)/shard_map/ppermute | solution.py:21
  123.0 15.1 %collective-permute-start.4 = (s32[256]{0:T(256)S(1)}, s32[256]{0:T(256)S(1)}, u32[]{:S(2)}, u32[]{:S(2)}) collective-permute-start(s32[256]{0:T(256)S(1)} %collective-permute-done.2), channel_id=1, source_target_pairs={{0,1},{1,2},{2,3},{3,4},{4,5},{5,6},{6,7},{7,8},{8,9},{9,10},{10,1... | collective-permute-start | bytes 3080 | tf_op jit(solution)/shard_map/ppermute | solution.py:18
  137.9 4.3 %collective-permute-start.5 = (s32[256]{0:T(256)S(1)}, s32[256]{0:T(256)S(1)}, u32[]{:S(2)}, u32[]{:S(2)}) collective-permute-start(s32[256]{0:T(256)S(1)} %collective-permute-done.3), channel_id=1, source_target_pairs={{0,15},{1,0},{2,1},{3,2},{4,3},{5,4},{6,5},{7,6},{8,7},{9,8},{10,9... | collective-permute-start | bytes 3080 | tf_op jit(solution)/shard_map/ppermute | solution.py:21
  138.1 4.3 %collective-permute-start.6 = (s32[256]{0:T(256)S(1)}, s32[256]{0:T(256)S(1)}, u32[]{:S(2)}, u32[]{:S(2)}) collective-permute-start(s32[256]{0:T(256)S(1)} %collective-permute-done.4), channel_id=1, source_target_pairs={{0,1},{1,2},{2,3},{3,4},{4,5},{5,6},{6,7},{7,8},{8,9},{9,10},{10,1... | collective-permute-start | bytes 3080 | tf_op jit(solution)/shard_map/ppermute | solution.py:18
  142.1 3.9 collective-permute-start.7
  142.4 3.9 collective-permute-start.8
  146.0 4.1 %collective-permute-start.9 = (s32[256]{0:T(256)S(1)}, s32[256]{0:T(256)S(1)}, u32[]{:S(2)}, u32[]{:S(2)}) collective-permute-start(s32[256]{0:T(256)S(1)} %collective-permute-done.7), channel_id=1, source_target_pairs={{0,15},{1,0},{2,1},{3,2},{4,3},{5,4},{6,5},{7,6},{8,7},{9,8},{10,9... | collective-permute-start | bytes 3080 | tf_op jit(solution)/shard_map/ppermute | solution.py:21
  146.3 3.9 collective-permute-start.10
  149.5 57.6 %copy-start.27 = (f32[4]{0:T(128)}, f32[4]{0:T(128)S(1)}, u32[]{:S(2)}) copy-start(f32[4]{0:T(128)S(1)} %dynamic_slice.103) | copy-start | bytes 52
  150.1 8.3 %collective-permute-start.11 = (s32[256]{0:T(256)S(1)}, s32[256]{0:T(256)S(1)}, u32[]{:S(2)}, u32[]{:S(2)}) collective-permute-start(s32[256]{0:T(256)S(1)} %collective-permute-done.9), channel_id=1, source_target_pairs={{0,15},{1,0},{2,1},{3,2},{4,3},{5,4},{6,5},{7,6},{8,7},{9,8},{10,9... | collective-permute-start | bytes 3080 | tf_op jit(solution)/shard_map/ppermute | solution.py:21
  150.2 8.3 %collective-permute-start.12 = (s32[256]{0:T(256)S(1)}, s32[256]{0:T(256)S(1)}, u32[]{:S(2)}, u32[]{:S(2)}) collective-permute-start(s32[256]{0:T(256)S(1)} %collective-permute-done.10), channel_id=1, source_target_pairs={{0,1},{1,2},{2,3},{3,4},{4,5},{5,6},{6,7},{7,8},{8,9},{9,10},{10,1... | collective-permute-start | bytes 3080 | tf_op jit(solution)/shard_map/ppermute | solution.py:18
  158.5 11.9 %collective-permute-start.13 = (s32[256]{0:T(256)S(1)}, s32[256]{0:T(256)S(1)}, u32[]{:S(2)}, u32[]{:S(2)}) collective-permute-start(s32[256]{0:T(256)S(1)} %collective-permute-done.11), channel_id=1, source_target_pairs={{0,15},{1,0},{2,1},{3,2},{4,3},{5,4},{6,5},{7,6},{8,7},{9,8},{10,9... | collective-permute-start | bytes 3080 | tf_op jit(solution)/shard_map/ppermute | solution.py:21
  158.5 12.1 %collective-permute-start.14 = (s32[256]{0:T(256)S(1)}, s32[256]{0:T(256)S(1)}, u32[]{:S(2)}, u32[]{:S(2)}) collective-permute-start(s32[256]{0:T(256)S(1)} %collective-permute-done.12), channel_id=1, source_target_pairs={{0,1},{1,2},{2,3},{3,4},{4,5},{5,6},{6,7},{7,8},{8,9},{9,10},{10,1... | collective-permute-start | bytes 3080 | tf_op jit(solution)/shard_map/ppermute | solution.py:18
  192.2 54.7 %all-to-all-start.1 = ((bf16[256,16,256]{0,2,1:T(8,128)(2,1)}), bf16[256,16,256]{0,2,1:T(8,128)(2,1)S(1)}, u32[]{:S(2)}, u32[]{:S(2)}) async-start(bf16[256,16,256]{0,2,1:T(8,128)(2,1)} %bitcast.244), calls=%async_computation.1 | async-start | bytes 4194304 | tf_op jit(solution)/shard_map/all_to_all | solution.py:200
  318.0 78.9 %all-to-all-start.4 = ((bf16[16,256,256]{1,2,0:T(8,128)(2,1)}), bf16[16,256,256]{1,2,0:T(8,128)(2,1)}, u32[]{:S(2)}, u32[]{:S(2)}) async-start(bf16[16,256,256]{1,2,0:T(8,128)(2,1)} %bitcast.255), calls=%async_computation.4 | async-start | bytes 4194304 | tf_op jit(solution)/shard_map/all_to_all | solution.py:237
  326.3 56.4 %copy-start.11 = (bf16[4096,128]{1,0:T(8,128)(2,1)S(1)}, bf16[4096,128]{1,0:T(8,128)(2,1)}, u32[]{:S(2)}) copy-start(bf16[4096,128]{1,0:T(8,128)(2,1)} %all-gather.6.cloned.1.call-done) | copy-start | bytes 3145732
  326.3 56.4 %copy-start.19 = (f32[16,256,4]{1,2,0:T(4,128)S(1)}, f32[16,256,4]{1,2,0:T(4,128)}, u32[]{:S(2)}) copy-start(f32[16,256,4]{1,2,0:T(4,128)} %copy-done.17) | copy-start | bytes 196612
  (27 other events, 260.6 us)
Sparse Core Ops, SparseCore 0:
  28.4 51.8 all-gather.5
  86.8 51.8 all-gather.3
